TPU v7x, 256 devices: a whole 4x4x8 slice. The times are simulated.
256 devices in a mesh: expert: 32 (over z, y), etp: 8 (over x, core).
Axes of the slice: x: 4, y: 4, z: 8, core: 2. Of those that a mesh axis runs over, the one named last changes fastest.
Arguments:
- tokens: bfloat16 [32768, 2560], P(('expert', 'etp')), may hold values from -6 to 6
- grad_out: bfloat16 [32768, 2560], P(('expert', 'etp')), may hold values from -6 to 6
- router_weight: bfloat16 [2560, 32], replicated, may hold values from -0.125 to 0.125
- expert_choice: int32 [32768, 1], P(('expert', 'etp')), may hold values from 0 to 31; in each aligned block of 128 rows (0 to 127, 128 to 255, ...) at most 6 rows name the same one
- gate_pre: bfloat16 [32, 1536, 4096], P('expert', None, 'etp'), may hold values from -6 to 6
- up_pre: bfloat16 [32, 1536, 4096], P('expert', None, 'etp'), may hold values from -6 to 6
- w_gate: bfloat16 [32, 2560, 4096], P('expert', None, 'etp'), may hold values from -0.125 to 0.125
- w_up: bfloat16 [32, 2560, 4096], P('expert', None, 'etp'), may hold values from -0.125 to 0.125
- w_down: bfloat16 [32, 4096, 2560], P('expert', 'etp'), may hold values from -0.09375 to 0.09375
Outputs:
- token_grad: bfloat16 [32768, 2560], P(('expert', 'etp'))
- router_grad: float32 [2560, 32], replicated
Inputs may be any that keep to these rules, and one draw needn't show every extreme that they name: `expert_choice`: within the 128 tokens of one device no expert is chosen more than 6 times, and in every draw some expert is chosen exactly 6 times by the tokens of some device.
All inputs are finite; a program needn't handle non-finite values.
Results may differ from a plain program's by a relative error of at most 0.015.
Values may be sent and summed in bfloat16 or wider, within the bound.
No kernel may reach another device: no remote copies, remote signals or barrier semaphores. Data moves between devices by JAX's collectives and lax.ppermute only.
A program may use at most 128 MiB of HBM per device.

v0:
```python
import jax
import jax.numpy as jnp
from jax import lax
from jax.sharding import PartitionSpec as P


def local(tokens, grad_out, router_weight, expert_choice, gate_pre, up_pre, w_gate, w_up, w_down):
    width = tokens.shape[1]
    experts = router_weight.shape[1]
    n_expert = lax.axis_size("expert")
    n_etp = lax.axis_size("etp")
    capacity = gate_pre.shape[1] // (n_expert * n_etp)
    hidden = w_down.shape[1]
    contract = (((1,), (1,)), ((), ()))
    chosen_ids = expert_choice[:, 0]
    picked = chosen_ids[:, None] == jnp.arange(experts, dtype=jnp.int32)[None, :]
    logits = jnp.dot(tokens, router_weight, preferred_element_type=jnp.float32)
    score = jax.nn.sigmoid(jnp.sum(jnp.where(picked, logits, 0.0), axis=1))
    counts = picked.astype(jnp.int32)
    earlier = jnp.cumsum(counts, axis=0) - counts
    position = jnp.sum(earlier * counts, axis=1)
    target = chosen_ids * capacity + position
    outgoing = jnp.zeros((experts * capacity, width), jnp.bfloat16).at[target].set(grad_out)
    gate_all = gate_pre[0]
    up_all = up_pre[0]
    gate_w = w_gate[0]
    up_w = w_up[0]
    down_w = w_down[0]
    pooled = lax.all_gather(outgoing, "etp", axis=0, tiled=True)
    pooled = pooled.reshape(n_etp, experts * capacity, width)
    arrived = lax.all_to_all(pooled, "expert", split_axis=1, concat_axis=1, tiled=True)
    d_hidden = lax.dot_general(
        arrived.reshape(n_etp * experts * capacity, width),
        down_w,
        contract,
        preferred_element_type=jnp.float32,
    )
    gate_f = gate_all.astype(jnp.float32)
    up_f = up_all.astype(jnp.float32)
    sig = jax.nn.sigmoid(gate_f)
    d_gate = (d_hidden * up_f * sig * (1.0 + gate_f * (1.0 - sig))).astype(jnp.bfloat16)
    d_up = (d_hidden * gate_f * sig).astype(jnp.bfloat16)
    both = jnp.concatenate([d_gate, d_up], axis=1)
    term = lax.dot_general(both[:, :hidden], gate_w, contract, preferred_element_type=jnp.float32)
    terms = (
        term + lax.dot_general(both[:, hidden:], up_w, contract, preferred_element_type=jnp.float32)
    ).astype(jnp.bfloat16)
    terms = terms.reshape(n_etp, experts * capacity, width)
    swapped = lax.all_to_all(terms, "expert", split_axis=1, concat_axis=1, tiled=True)
    summed = lax.psum_scatter(swapped, "etp", scatter_dimension=0, tiled=True).astype(jnp.float32)
    returned = summed.reshape(experts * capacity, width).astype(jnp.bfloat16)
    fetched = returned[target].astype(jnp.float32)
    inputs = tokens.astype(jnp.float32)
    d_logit = jnp.sum(inputs * fetched, axis=1) * score * (1.0 - score)
    column = lax.dot_general(
        picked.astype(jnp.bfloat16), router_weight, contract, preferred_element_type=jnp.float32
    )
    token_grad = (score[:, None] * fetched + d_logit[:, None] * column).astype(jnp.bfloat16)
    weighted = jnp.where(picked, d_logit[:, None], 0.0)
    local_terms = jnp.dot(
        inputs.T, weighted, precision=lax.Precision.HIGHEST, preferred_element_type=jnp.float32
    )
    router_grad = lax.psum(local_terms, ("expert", "etp"))
    return (token_grad, router_grad)


def solution(mesh):
    placed = (
        P(("expert", "etp"), None),
        P(("expert", "etp"), None),
        P(),
        P(("expert", "etp"), None),
        P("expert", None, "etp"),
        P("expert", None, "etp"),
        P("expert", None, "etp"),
        P("expert", None, "etp"),
        P("expert", "etp", None),
    )
    return jax.shard_map(
        local,
        mesh=mesh,
        in_specs=placed,
        out_specs=(P(("expert", "etp"), None), P()),
        check_vma=False,
    )
```

profile of v0, /device:TPU:6, one launch (start us, length us, event | category | flops | bytes accessed | tf_op | source)
XLA Modules:
  0.0 810.6 jit_solution(2076231841087327123)
XLA Ops:
  7.2 0.0 copy-start
  7.2 0.0 all-gather.2.cloned.1.call-start
  7.2 0.8 fusion.28
  8.0 0.1 copy.20
  8.1 0.2 reduce_window_sum.11
  8.3 0.1 copy.21
  8.4 0.7 select_reduce_fusion
  9.1 0.7 fusion.33
  9.7 3.2 scatter_custom_fusion
  12.9 0.0 all-gather.2.cloned.1.call-update
  13.0 0.0 reduce-scatter.2.cloned.1.call-start
  13.0 51.2 %all-gather.2.cloned.1.call-done = bf16[1536,2560]{1,0:T(8,128)(2,1)} async-done(((bf16[192,2560]{1,0:T(8,128)(2,1)}), bf16[1536,2560]{1,0:T(8,128)(2,1)}) %all-gather.2.cloned.1.call-update) | async-done | bytes 7864336 | tf_op jit(solution)/shard_map/all_gather | solution.py:29
  64.2 10.7 %copy.22 = bf16[8,192,2560]{2,0,1:T(8,128)(2,1)} copy(bf16[8,192,2560]{2,1,0:T(8,128)(2,1)} %bitcast.44) | data formatting | bytes 15728640 | tf_op jit(solution)/shard_map/reshape | solution.py:30
  74.9 185.5 %all_to_all.10 = bf16[8,192,2560]{2,0,1:T(8,128)(2,1)} all-to-all(bf16[8,192,2560]{2,0,1:T(8,128)(2,1)} %copy.22), channel_id=1, replica_groups=mesh['expert'=32,'etp'=8] {'expert'}, dimensions={1} | all-to-all | bytes 15728640 | tf_op jit(solution)/shard_map/all_to_all | solution.py:31
  260.4 0.0 copy-start.5
  260.4 9.0 %copy.23 = bf16[8,192,2560]{2,1,0:T(8,128)(2,1)} copy(bf16[8,192,2560]{2,0,1:T(8,128)(2,1)} %all_to_all.10) | data formatting | bytes 15728640 | tf_op jit(solution)/shard_map/all_to_all | solution.py:31
  269.4 0.0 copy-done.5
  269.4 0.0 copy-start.6
  269.4 0.0 copy-start.7
  269.4 6.7 fusion.14
  276.1 0.0 copy-start.8
  276.1 1.7 copy-done.8
  277.8 0.0 copy-done
  277.8 0.0 copy-done.6
  277.8 0.0 copy-done.7
  277.8 9.9 %fusion.12 = f32[1536,2560]{1,0:T(8,128)} fusion(bf16[1,2560,512]{2,1,0:T(8,128)(2,1)S(1)} %copy-done, f32[1536,512]{1,0:T(8,128)S(1)} %fusion.14, bf16[1,1536,512]{2,1,0:T(8,128)(2,1)S(1)} %copy-done.6, bf16[1,1536,512]{2,1,0:T(8,128)(2,1)S(1)} %copy-done.7), kind=kOutput, calls=%fused_computation.21 | convolution fusion | flops 4035969024 | bytes 24641536 | tf_op jit(solution)/shard_map/dot_general | solution.py:44
  287.7 15.2 %add_convert_fusion = bf16[1536,2560]{1,0:T(8,128)(2,1)} fusion(f32[1536,2560]{1,0:T(8,128)} %fusion.12, bf16[1,2560,512]{2,1,0:T(8,128)(2,1)} %param.16, f32[1536,512]{1,0:T(8,128)} %copy-done.8, bf16[1,1536,512]{2,1,0:T(8,128)(2,1)} %param.13), kind=kOutput, calls=%fused_computation.2 | convolution fusion | flops 4039901184 | bytes 30932992 | tf_op jit(solution)/shard_map/dot_general | solution.py:46
  303.0 10.6 %copy.24 = bf16[8,192,2560]{2,0,1:T(8,128)(2,1)} copy(bf16[8,192,2560]{2,1,0:T(8,128)(2,1)} %bitcast.45) | data formatting | bytes 15728640 | tf_op jit(solution)/shard_map/reshape | solution.py:48
  313.6 179.1 %all_to_all.11 = bf16[8,192,2560]{2,0,1:T(8,128)(2,1)} all-to-all(bf16[8,192,2560]{2,0,1:T(8,128)(2,1)} %copy.24), channel_id=1, replica_groups=mesh['expert'=32,'etp'=8] {'expert'}, dimensions={1} | all-to-all | bytes 15728640 | tf_op jit(solution)/shard_map/all_to_all | solution.py:49
  492.7 8.7 %copy.25 = bf16[8,192,2560]{2,1,0:T(8,128)(2,1)} copy(bf16[8,192,2560]{2,0,1:T(8,128)(2,1)} %all_to_all.11) | data formatting | bytes 15728640 | tf_op jit(solution)/shard_map/all_to_all | solution.py:49
  501.5 0.0 copy-start.2
  501.5 0.0 copy-start.3
  501.5 0.0 copy-start.4
  501.5 0.0 reduce-scatter.2.cloned.1.call-update
  501.5 0.0 all-reduce.2.cloned.1.call-start
  501.6 1.0 copy-done.2
  502.6 0.0 copy-done.3
  502.6 0.0 copy-done.4
  502.6 0.3 fusion.24
  502.9 46.1 %reduce-scatter.2.cloned.1.call-done = bf16[1,192,2560]{2,1,0:T(8,128)(2,1)} async-done(((bf16[8,192,2560]{2,1,0:T(8,128)(2,1)}), bf16[1,192,2560]{2,1,0:T(8,128)(2,1)}) %reduce-scatter.2.cloned.1.call-update) | async-done | bytes 983056 | tf_op jit(solution)/shard_map/reduce_scatter | solution.py:50
  549.0 3.9 gather_fusion
  553.0 1.3 fusion.23
  554.3 1.1 convolution_bitcast_fusion
  555.4 0.0 all-reduce.2.cloned.1.call-update
  555.5 2.3 fusion.1
  557.8 244.6 %all-reduce.2.cloned.1.call-done = f32[2560,32]{0,1:T(8,128)} async-done(((f32[2560,32]{0,1:T(8,128)}), f32[2560,32]{0,1:T(8,128)}) %all-reduce.2.cloned.1.call-update) | async-done | bytes 327696 | tf_op jit(solution)/shard_map/psum | solution.py:63
  802.4 1.7 copy.27
  804.1 0.0 copy-done.1
  (3 shorter events, 0.0 us)
Async XLA Ops:
  7.2 270.7 %copy-start = (bf16[1,2560,512]{2,1,0:T(8,128)(2,1)S(1)}, bf16[1,2560,512]{2,1,0:T(8,128)(2,1)}, u32[]{:S(2)}) copy-start(bf16[1,2560,512]{2,1,0:T(8,128)(2,1)} %param.15) | copy-start | bytes 7864324
  7.2 57.0 %all-gather.2.cloned.1.call-start = ((), (), s32[]{:S(2)}) async-start(), calls=%async_computation.3 | async-start | bytes 8847360 | tf_op jit(solution)/shard_map/all_gather | solution.py:29
  13.0 536.1 %reduce-scatter.2.cloned.1.call-start = ((), (), s32[]{:S(2)}) async-start(), calls=%async_computation.4 | async-start | bytes 8847360 | tf_op jit(solution)/shard_map/reduce_scatter | solution.py:50
  260.4 9.0 %copy-start.5 = (bf16[1,512,2560]{2,1,0:T(8,128)(2,1)S(1)}, bf16[1,512,2560]{2,1,0:T(8,128)(2,1)}, u32[]{:S(2)}) copy-start(bf16[1,512,2560]{2,1,0:T(8,128)(2,1)} %param.17) | copy-start | bytes 7864324
  269.4 8.5 %copy-start.6 = (bf16[1,1536,512]{2,1,0:T(8,128)(2,1)S(1)}, bf16[1,1536,512]{2,1,0:T(8,128)(2,1)}, u32[]{:S(2)}) copy-start(bf16[1,1536,512]{2,1,0:T(8,128)(2,1)} %param.14) | copy-start | bytes 4718596
  269.4 8.5 %copy-start.7 = (bf16[1,1536,512]{2,1,0:T(8,128)(2,1)S(1)}, bf16[1,1536,512]{2,1,0:T(8,128)(2,1)}, u32[]{:S(2)}) copy-start(bf16[1,1536,512]{2,1,0:T(8,128)(2,1)} %param.13) | copy-start | bytes 4718596
  276.1 1.7 copy-start.8
  501.5 1.1 copy-start.2
  501.5 1.1 copy-start.3
  501.5 1.1 copy-start.4
  501.5 300.9 %all-reduce.2.cloned.1.call-start = ((), (), s32[]{:S(2)}) async-start(), calls=%async_computation.5 | async-start | bytes 655360 | tf_op jit(solution)/shard_map/psum | solution.py:63
  549.0 255.1 %copy-start.1 = (bf16[1,2560,512]{2,1,0:T(8,128)(2,1)S(1)}, bf16[1,2560,512]{2,1,0:T(8,128)(2,1)}, u32[]{:S(2)}) copy-start(bf16[1,2560,512]{2,1,0:T(8,128)(2,1)} %param.15) | copy-start | bytes 7864324
Sparse Core Ops, SparseCore 0:
  13.1 51.0 all-gather.1
  501.6 47.3 reduce-scatter.1
  555.6 246.7 all-reduce.1
where the time goes:
time: 813 us; the launch traced here: 811 us
  blocking collectives  365 us (45%)
  waiting for transfers between devices  342 us (42%)
  local copies, waits for them, and re-layouts  50.8 us (6%)
  matrix products  35.6 us (4%)
  between operations  13.8 us (2%)
    psum x1, waiting for transfers between devices, local(): router_grad = lax.psum(local_terms, ('expert', 'etp'))  245 us
    all_to_all x1, blocking collectives, local(): lax.all_to_all(pooled, 'expert', split_axis=1, concat_axis=1, tiled=True)  185 us
    all_to_all x1, blocking collectives, local(): lax.all_to_all(terms, 'expert', split_axis=1, concat_axis=1, tiled=True)  179 us
    all_gather x1, waiting for transfers between devices, local(): pooled = lax.all_gather(outgoing, 'etp', axis=0, tiled=True)  51.2 us
    reduce_scatter x1, waiting for transfers between devices, local(): lax.psum_scatter(swapped, 'etp', scatter_dimension=0, tiled=True)  46.1 us
  transfers between devices with their start and end apart: 3, of which 3 were waited for; matrix products, arithmetic and copies ran while one was open for 0% of the time, Pallas kernels for 0%

commit v1 on v0

v1 whole, which is shorter than its diff:
```python
import jax
import jax.numpy as jnp
from jax import lax
from jax.sharding import PartitionSpec as P


def local(tokens, grad_out, router_weight, expert_choice, gate_pre, up_pre, w_gate, w_up, w_down):
    width = tokens.shape[1]
    experts = router_weight.shape[1]
    n_expert = lax.axis_size("expert")
    n_etp = lax.axis_size("etp")
    capacity = gate_pre.shape[1] // (n_expert * n_etp)
    contract = (((1,), (1,)), ((), ()))
    chosen_ids = expert_choice[:, 0]
    picked = chosen_ids[:, None] == jnp.arange(experts, dtype=jnp.int32)[None, :]
    logits = jnp.dot(tokens, router_weight, preferred_element_type=jnp.float32)
    score = jax.nn.sigmoid(jnp.sum(jnp.where(picked, logits, 0.0), axis=1))
    counts = picked.astype(jnp.int32)
    earlier = jnp.cumsum(counts, axis=0) - counts
    position = jnp.sum(earlier * counts, axis=1)
    target = chosen_ids * capacity + position
    placed = jnp.arange(experts * capacity, dtype=jnp.int32)[:, None] == target[None, :]
    onehot = placed.astype(jnp.bfloat16)
    outgoing = jnp.dot(onehot, grad_out, preferred_element_type=jnp.float32).astype(jnp.bfloat16)
    own = lax.all_to_all(outgoing, "expert", split_axis=0, concat_axis=0, tiled=True)
    arrived = lax.all_gather(own, "etp", axis=0, tiled=True)
    d_hidden = lax.dot_general(arrived, w_down[0], contract, preferred_element_type=jnp.float32)
    gate_f = gate_pre[0].astype(jnp.float32)
    up_f = up_pre[0].astype(jnp.float32)
    sig = jax.nn.sigmoid(gate_f)
    d_gate = (d_hidden * up_f * sig * (1.0 + gate_f * (1.0 - sig))).astype(jnp.bfloat16)
    d_up = (d_hidden * gate_f * sig).astype(jnp.bfloat16)
    terms = (
        lax.dot_general(d_gate, w_gate[0], contract, preferred_element_type=jnp.float32)
        + lax.dot_general(d_up, w_up[0], contract, preferred_element_type=jnp.float32)
    ).astype(jnp.bfloat16)
    summed = lax.psum_scatter(terms, "etp", scatter_dimension=0, tiled=True)
    returned = lax.all_to_all(summed, "expert", split_axis=0, concat_axis=0, tiled=True)
    fetched = lax.dot_general(
        onehot, returned, (((0,), (0,)), ((), ())), preferred_element_type=jnp.float32
    )
    inputs = tokens.astype(jnp.float32)
    d_logit = jnp.sum(inputs * fetched, axis=1) * score * (1.0 - score)
    column = lax.dot_general(
        picked.astype(jnp.bfloat16), router_weight, contract, preferred_element_type=jnp.float32
    )
    token_grad = (score[:, None] * fetched + d_logit[:, None] * column).astype(jnp.bfloat16)
    weighted = jnp.where(picked, d_logit[:, None], 0.0)
    local_terms = lax.dot_general(
        weighted, inputs, (((0,), (0,)), ((), ())), precision=lax.Precision.HIGHEST, preferred_element_type=jnp.float32
    )
    mine = lax.all_to_all(local_terms.reshape(n_etp, experts // n_etp, width), "etp", split_axis=0, concat_axis=0, tiled=True)
    mine = jnp.sum(mine, axis=0)
    mine = lax.psum(mine, "expert")
    router_grad = lax.all_gather(mine, "etp", axis=0, tiled=True).T
    return (token_grad, router_grad)


def solution(mesh):
    placed = (
        P(("expert", "etp"), None),
        P(("expert", "etp"), None),
        P(),
        P(("expert", "etp"), None),
        P("expert", None, "etp"),
        P("expert", None, "etp"),
        P("expert", None, "etp"),
        P("expert", None, "etp"),
        P("expert", "etp", None),
    )
    return jax.shard_map(
        local,
        mesh=mesh,
        in_specs=placed,
        out_specs=(P(("expert", "etp"), None), P()),
        check_vma=False,
    )
```

time: 813 us -> 424 us (0.52)
  waiting for transfers between devices: 342 us -> 134 us
  blocking collectives: 365 us -> 200 us
  local copies, waits for them, and re-layouts: 50.8 us -> 13.6 us
  starting transfers between devices: 0.12 us -> 15 us
    all_to_all x2 -> x1, blocking collectives: 365 us -> 46.8 us  [local(): lax.all_to_all(outgoing, 'expert', split_axis=0, concat_axis=0, tiled=True)]
    psum x1 -> x0, waiting for transfers between devices: 245 us -> none  [local(): router_grad = lax.psum(local_terms, ('expert', 'etp'))]
    psum x0 -> x1, blocking collectives: none -> 140 us  [local(): mine = lax.psum(mine, 'expert')]
    all_to_all x0 -> x2, waiting for transfers between devices: none -> 37.2 us  [the longest x1 33.6 us: local(): lax.all_to_all(summed, 'expert', split_axis=0, concat_axis=0, tiled=True)]
    reshape x2 -> x1, local copies, waits for them, and re-layouts: 21.3 us -> 1.81 us  [local(): local_terms.reshape(n_etp, experts // n_etp, width)]
    all_to_all x0 -> x2, starting transfers between devices: none -> 14.9 us  [the longest x1 9.97 us: local(): lax.all_to_all(summed, 'expert', split_axis=0, concat_axis=0, tiled=True)]
    all_gather x0 -> x1, blocking collectives: none -> 12.9 us  [local(): router_grad = lax.all_gather(mine, 'etp', axis=0, tiled=True).T]
    all_to_all x2 -> x4, local copies, waits for them, and re-layouts: 17.7 us -> 9.07 us  [the longest x2 4.56 us: local(): lax.all_to_all(outgoing, 'expert', split_axis=0, concat_axis=0, tiled=True)]
  transfers between devices with their start and end apart: 3 -> 4, of which waited for: 3 -> 4; matrix products, arithmetic and copies ran while one was open for 0% -> 1% of each run, Pallas kernels for 0% -> 0%
where the time goes in v1:
time: 424 us; the launch traced here: 420 us
  blocking collectives  200 us (47%)
  waiting for transfers between devices  134 us (32%)
  matrix products  41.7 us (10%)
  starting transfers between devices  15 us (4%)
  between operations  14.1 us (3%)
  local copies, waits for them, and re-layouts  13.6 us (3%)
    psum x1, blocking collectives, local(): mine = lax.psum(mine, 'expert')  140 us
    reduce_scatter x1, waiting for transfers between devices, local(): summed = lax.psum_scatter(terms, 'etp', scatter_dimension=0, tiled=True)  52.8 us
    all_to_all x1, blocking collectives, local(): lax.all_to_all(outgoing, 'expert', split_axis=0, concat_axis=0, tiled=True)  46.8 us
    all_gather x1, waiting for transfers between devices, local(): arrived = lax.all_gather(own, 'etp', axis=0, tiled=True)  43.7 us
    all_to_all x1, waiting for transfers between devices, local(): lax.all_to_all(summed, 'expert', split_axis=0, concat_axis=0, tiled=True)  33.6 us
    dot_general x1, matrix products, local(): lax.dot_general(d_up, w_up[0], contract, preferred_element_type=jnp.float32)  15.2 us
    all_gather x1, blocking collectives, local(): router_grad = lax.all_gather(mine, 'etp', axis=0, tiled=True).T  12.9 us
    all_to_all x1, starting transfers between devices, local(): lax.all_to_all(summed, 'expert', split_axis=0, concat_axis=0, tiled=True)  9.97 us
  transfers between devices with their start and end apart: 4, of which 4 were waited for; matrix products, arithmetic and copies ran while one was open for 1% of the time, Pallas kernels for 0%

profile of v1, /device:TPU:6, one launch (start us, length us, event | category | flops | bytes accessed | tf_op | source)
XLA Modules:
  0.0 420.2 jit_solution(13606596880845416231)
XLA Ops:
  7.2 0.0 copy-start
  7.2 0.0 all-gather.3.cloned.1.call-start
  7.2 0.8 fusion.29
  8.0 0.1 copy.15
  8.1 0.2 reduce_window_sum.11
  8.3 0.1 copy.16
  8.4 0.7 select_reduce_fusion
  9.1 0.7 multiply_add_fusion
  9.7 2.5 convolution_convert_fusion
  12.2 2.3 all_to_all.19
  14.5 46.8 %all_to_all.29 = bf16[32,6,2560]{2,1,0:T(8,128)(2,1)} all-to-all(bf16[32,6,2560]{2,1,0:T(8,128)(2,1)} %all_to_all.19), channel_id=1, replica_groups=mesh['expert'=32,'etp'=8] {'expert'}, dimensions={0} | all-to-all | bytes 1966080 | tf_op jit(solution)/shard_map/all_to_all | solution.py:25
  61.3 2.3 all_to_all.21
  63.6 0.0 all-gather.3.cloned.1.call-update
  63.6 0.0 reduce-scatter.2.cloned.1.call-start
  63.7 43.7 %all-gather.3.cloned.1.call-done = bf16[1536,2560]{1,0:T(8,128)(2,1)} async-done(((bf16[192,2560]{1,0:T(8,128)(2,1)}), bf16[1536,2560]{1,0:T(8,128)(2,1)}) %all-gather.3.cloned.1.call-update) | async-done | bytes 7864336 | tf_op jit(solution)/shard_map/all_gather | solution.py:26
  107.4 0.0 copy-start.4
  107.4 0.0 copy-start.5
  107.4 7.5 %fusion.14 = f32[1536,512]{1,0:T(8,128)S(1)} fusion(bf16[1536,2560]{1,0:T(8,128)(2,1)} %all-gather.3.cloned.1.call-done, bf16[1,512,2560]{2,1,0:T(8,128)(2,1)} %param.17), kind=kOutput, calls=%fused_computation.21 | convolution fusion | flops 4026531840 | bytes 13631488 | tf_op jit(solution)/shard_map/dot_general | solution.py:27
  114.9 0.0 copy-start.6
  115.0 1.7 copy-done.6
  116.7 0.0 copy-done
  116.7 0.0 copy-done.4
  116.7 0.0 copy-done.5
  116.7 9.8 %fusion.12 = f32[1536,2560]{1,0:T(8,128)} fusion(bf16[1,2560,512]{2,1,0:T(8,128)(2,1)S(1)} %copy-done, f32[1536,512]{1,0:T(8,128)S(1)} %fusion.14, bf16[1,1536,512]{2,1,0:T(8,128)(2,1)S(1)} %copy-done.4, bf16[1,1536,512]{2,1,0:T(8,128)(2,1)S(1)} %copy-done.5), kind=kOutput, calls=%fused_computation.19 | convolution fusion | flops 4035969024 | bytes 24641536 | tf_op jit(solution)/shard_map/dot_general | solution.py:34
  126.5 15.2 %add_convert_fusion = bf16[1536,2560]{1,0:T(8,128)(2,1)} fusion(f32[1536,2560]{1,0:T(8,128)} %fusion.12, bf16[1,2560,512]{2,1,0:T(8,128)(2,1)} %param.16, f32[1536,512]{1,0:T(8,128)} %copy-done.6, bf16[1,1536,512]{2,1,0:T(8,128)(2,1)} %param.13), kind=kOutput, calls=%fused_computation | convolution fusion | flops 4039901184 | bytes 30932992 | tf_op jit(solution)/shard_map/dot_general | solution.py:35
  141.7 0.0 reduce-scatter.2.cloned.1.call-update
  141.8 0.0 copy-start.1
  141.8 0.0 copy-start.2
  141.8 0.0 copy-start.3
  141.8 52.8 %reduce-scatter.2.cloned.1.call-done = bf16[192,2560]{1,0:T(8,128)(2,1)} async-done(((bf16[1536,2560]{1,0:T(8,128)(2,1)}), bf16[192,2560]{1,0:T(8,128)(2,1)}) %reduce-scatter.2.cloned.1.call-update) | async-done | bytes 983056 | tf_op jit(solution)/shard_map/reduce_scatter | solution.py:37
  194.6 2.3 all_to_all.22
  196.8 10.0 %all-to-all-start.1 = ((bf16[32,6,2560]{2,1,0:T(8,128)(2,1)}), bf16[32,6,2560]{2,1,0:T(8,128)(2,1)}, u32[]{:S(2)}, u32[]{:S(2)}) async-start(bf16[32,6,2560]{2,1,0:T(8,128)(2,1)} %all_to_all.22), calls=%async_computation.2 | async-start | bytes 2621440 | tf_op jit(solution)/shard_map/all_to_all | solution.py:38
  206.8 0.0 copy-done.1
  206.8 0.0 copy-done.2
  206.8 0.0 copy-done.3
  206.8 0.3 fusion.23
  207.2 33.6 %all-to-all-done.1 = bf16[32,6,2560]{2,1,0:T(8,128)(2,1)} async-done(((bf16[32,6,2560]{2,1,0:T(8,128)(2,1)}), bf16[32,6,2560]{2,1,0:T(8,128)(2,1)}, u32[]{:S(2)}, u32[]{:S(2)}) %all-to-all-start.1) | async-done | bytes 983072 | tf_op jit(solution)/shard_map/all_to_all | solution.py:38
  240.8 2.2 all_to_all.24
  243.0 2.7 multiply_reduce_fusion
  245.7 1.1 fusion.27
  246.8 1.8 reshape.36
  248.6 5.0 %all-to-all-start.2 = ((f32[8,4,2560]{2,1,0:T(4,128)}), f32[8,4,2560]{2,1,0:T(4,128)S(1)}, u32[]{:S(2)}, u32[]{:S(2)}) async-start(f32[8,4,2560]{2,1,0:T(4,128)} %reshape.36), calls=%async_computation.3 | async-start | bytes 655360 | tf_op jit(solution)/shard_map/all_to_all | solution.py:52
  253.6 2.5 fusion.1
  256.1 3.6 all-to-all-done.2
  259.7 0.1 reduce_sum.39
  259.8 139.8 %psum.7 = f32[4,2560]{1,0:T(4,128)S(1)} all-reduce(f32[4,2560]{1,0:T(4,128)S(1)} %reduce_sum.39), channel_id=1, replica_groups=mesh['expert'=32,'etp'=8] {'expert'}, use_global_device_ids=true, to_apply=%region_6.7 | all-reduce | flops 10240 | bytes 81920 | tf_op jit(solution)/shard_map/psum | solution.py:54
  399.6 12.9 %all-gather = f32[8,4,2560]{2,1,0:T(4,128)S(1)} all-gather(f32[1,4,2560]{2,1,0:T(4,128)S(1)} %bitcast.37), channel_id=1, replica_groups=mesh['expert'=32,'etp'=8] {'etp'}, dimensions={0}, use_global_device_ids=true | all-gather | bytes 368640 | tf_op jit(solution)/shard_map/all_gather | solution.py:55
  412.5 0.8 reshape.40
  (1 shorter events, 0.0 us)
Async XLA Ops:
  7.2 109.5 %copy-start = (bf16[1,2560,512]{2,1,0:T(8,128)(2,1)S(1)}, bf16[1,2560,512]{2,1,0:T(8,128)(2,1)}, u32[]{:S(2)}) copy-start(bf16[1,2560,512]{2,1,0:T(8,128)(2,1)} %param.15) | copy-start | bytes 7864324
  7.2 100.2 %all-gather.3.cloned.1.call-start = ((), (), s32[]{:S(2)}) async-start(), calls=%async_computation.4 | async-start | bytes 8847360 | tf_op jit(solution)/shard_map/all_gather | solution.py:26
  63.6 131.0 %reduce-scatter.2.cloned.1.call-start = ((), (), s32[]{:S(2)}) async-start(), calls=%async_computation.5 | async-start | bytes 8847360 | tf_op jit(solution)/shard_map/reduce_scatter | solution.py:37
  107.4 9.3 %copy-start.4 = (bf16[1,1536,512]{2,1,0:T(8,128)(2,1)S(1)}, bf16[1,1536,512]{2,1,0:T(8,128)(2,1)}, u32[]{:S(2)}) copy-start(bf16[1,1536,512]{2,1,0:T(8,128)(2,1)} %param.14) | copy-start | bytes 4718596
  107.4 9.3 %copy-start.5 = (bf16[1,1536,512]{2,1,0:T(8,128)(2,1)S(1)}, bf16[1,1536,512]{2,1,0:T(8,128)(2,1)}, u32[]{:S(2)}) copy-start(bf16[1,1536,512]{2,1,0:T(8,128)(2,1)} %param.13) | copy-start | bytes 4718596
  114.9 1.7 copy-start.6
  141.8 65.1 %copy-start.1 = (bf16[128,2560]{1,0:T(8,128)(2,1)S(1)}, bf16[128,2560]{1,0:T(8,128)(2,1)}, u32[]{:S(2)}) copy-start(bf16[128,2560]{1,0:T(8,128)(2,1)} %param.9) | copy-start | bytes 1966084
  141.8 65.1 %copy-start.2 = (bf16[2560,32]{0,1:T(8,128)(2,1)S(1)}, bf16[2560,32]{0,1:T(8,128)(2,1)}, u32[]{:S(2)}) copy-start(bf16[2560,32]{0,1:T(8,128)(2,1)} %param.11) | copy-start | bytes 491524
  141.8 65.1 %copy-start.3 = (s32[128,1]{0,1:T(1,128)S(1)}, s32[128,1]{0,1:T(1,128)}, u32[]{:S(2)}) copy-start(s32[128,1]{0,1:T(1,128)} %param.12) | copy-start | bytes 1540
  196.8 43.9 %all-to-all-start.1 = ((bf16[32,6,2560]{2,1,0:T(8,128)(2,1)}), bf16[32,6,2560]{2,1,0:T(8,128)(2,1)}, u32[]{:S(2)}, u32[]{:S(2)}) async-start(bf16[32,6,2560]{2,1,0:T(8,128)(2,1)} %all_to_all.22), calls=%async_computation.2 | async-start | bytes 2621440 | tf_op jit(solution)/shard_map/all_to_all | solution.py:38
  248.6 11.1 %all-to-all-start.2 = ((f32[8,4,2560]{2,1,0:T(4,128)}), f32[8,4,2560]{2,1,0:T(4,128)S(1)}, u32[]{:S(2)}, u32[]{:S(2)}) async-start(f32[8,4,2560]{2,1,0:T(4,128)} %reshape.36), calls=%async_computation.3 | async-start | bytes 655360 | tf_op jit(solution)/shard_map/all_to_all | solution.py:52
Sparse Core Ops, SparseCore 0:
  63.7 43.6 all-gather.2
  141.9 52.6 reduce-scatter.1
